TPU v7x, 256 devices: a whole 4x4x8 slice. The times are simulated.
256 devices in a mesh: ctx: 32 (over x, z), tp: 8 (over y, core).
Axes of the slice: x: 4, y: 4, z: 8, core: 2. Of those that a mesh axis runs over, the one named last changes fastest.
Arguments:
- projected: bfloat16 [4096, 3, 4096], P('ctx', None, 'tp'), may hold values from -6 to 6
- short_filter: float32 [7, 3, 4096], P(None, None, 'tp'), may hold values from -2.4 to 2.4
- long_filter: bfloat16 [256, 2048], P('tp'), may hold values from -0.26516504 to 0.26516504
- out_weight: bfloat16 [4096, 8192], P('tp'), may hold values from -0.09375 to 0.09375
Outputs:
- layer_out: bfloat16 [4096, 8192], P('ctx', 'tp')
All inputs are finite; a program needn't handle non-finite values.
Results may differ from a plain program's by a relative error of at most 0.015.
Values may be sent and summed in bfloat16 or wider, within the bound.
No kernel may reach another device: no remote copies, remote signals or barrier semaphores. Data moves between devices by JAX's collectives and lax.ppermute only.
A program may use at most 64 MiB of HBM per device.

v0:
```python
import math
import jax
import jax.numpy as jnp
from jax import lax
from jax.sharding import PartitionSpec as P


def shifted(array, axis, by):
    size = lax.axis_size(axis)
    pairs = [(i, i + by) for i in range(size) if 0 <= i + by < size]
    return lax.ppermute(array, axis, pairs)


def toeplitz_block(padded_taps, lag_base, count, tok_rows):
    width = tok_rows + count - 1
    groups = padded_taps.shape[0]
    window = lax.dynamic_slice_in_dim(padded_taps, lag_base - (count - 1) + 2 * tok_rows, width, 1)
    flipped = jnp.concatenate([window[:, ::-1], jnp.zeros((groups, 1), window.dtype)], axis=1)
    tiled = jnp.tile(flipped, (1, tok_rows))
    skewed = tiled[:, : tok_rows * width].reshape(groups, tok_rows, width)
    return skewed[:, :, tok_rows - 1 : tok_rows - 1 + count]


def block_term(padded_taps, source, lag_base, tok_rows):
    count, channels = source.shape
    groups = padded_taps.shape[0]
    matrix = toeplitz_block(padded_taps, lag_base, count, tok_rows)
    grouped = source.reshape(count, groups, channels // groups)
    term = jnp.einsum("gts,sgi->tgi", matrix, grouped, preferred_element_type=jnp.float32)
    return term.reshape(tok_rows, channels)


def add_blocks(total, piece, padded_taps, my_start, reach):
    tok_rows = total.shape[0]
    count = piece.shape[0]
    block = math.gcd(count, tok_rows)

    def one_block(index, carry):
        first = index * block
        source = lax.dynamic_slice_in_dim(piece, index * block, block, 0)
        lag_base = my_start - first
        useful = jnp.logical_and(lag_base + tok_rows - 1 >= 0, lag_base - block + 1 <= reach - 1)
        return lax.cond(
            useful,
            lambda running: running + block_term(padded_taps, source, lag_base, tok_rows),
            lambda running: running,
            carry,
        )

    return lax.fori_loop(0, count // block, one_block, total)


def body(projected, short_filter, long_filter, out_weight):
    tok_rows = projected.shape[0]
    taps = short_filter.shape[0]
    groups = long_filter.shape[0]
    reach = long_filter.shape[1]
    my_start = lax.axis_index("ctx") * tok_rows
    border = shifted(projected[tok_rows - (taps - 1) :], "ctx", 1)
    extended = jnp.concatenate([border, projected], axis=0).astype(jnp.float32)
    conved = short_filter[0] * extended[taps - 1 : taps - 1 + tok_rows]
    for offset in range(1, taps):
        conved = (
            conved
            + short_filter[offset] * extended[taps - 1 - offset : taps - 1 - offset + tok_rows]
        )
    values = (conved[:, 1, :] * conved[:, 2, :]).astype(jnp.bfloat16)
    padding = jnp.zeros((groups, 2 * tok_rows), long_filter.dtype)
    padded_taps = jnp.concatenate([padding, long_filter, padding], axis=1)
    empty = jnp.zeros(values.shape, jnp.float32)
    mixed = add_blocks(
        empty, lax.all_gather(values, "ctx", axis=0, tiled=True), padded_taps, my_start, reach
    )
    hidden = (conved[:, 0, :] * mixed).astype(jnp.bfloat16)
    partial_sum = jnp.dot(hidden, out_weight, preferred_element_type=jnp.float32)
    return lax.psum_scatter(partial_sum.astype(jnp.bfloat16), "tp", scatter_dimension=1, tiled=True)


def solution(mesh):
    return jax.shard_map(
        body,
        mesh=mesh,
        in_specs=(P("ctx", None, "tp"), P(None, None, "tp"), P("tp", None), P("tp", None)),
        out_specs=P("ctx", "tp"),
        check_vma=False,
    )
```

profile of v0, /device:TPU:2, one launch (start us, length us, event | category | flops | bytes accessed | tf_op | source)
XLA Modules:
  0.0 382.6 jit_solution(14550529410399828677)
XLA Ops:
  6.5 0.7 slice.63
  7.3 0.3 copy.7
  7.5 3.8 collective-permute-start
  11.4 1.2 fusion.12
  12.6 1.2 copy.8
  13.9 10.5 %collective-permute-done = bf16[6,3,512]{0,2,1:T(8,128)(2,1)S(1)} collective-permute-done((bf16[6,3,512]{0,2,1:T(8,128)(2,1)S(1)}, bf16[6,3,512]{0,2,1:T(8,128)(2,1)S(1)}, u32[]{:S(2)}, u32[]{:S(2)}) %collective-permute-start) | collective-permute-done | bytes 18464 | tf_op jit(solution)/shard_map/ppermute | solution.py:11
  24.4 0.3 maximum_convert_fusion
  24.7 3.0 fusion.2
  27.7 0.7 fusion.8
  28.5 83.2 %all-gather.3.cloned.1.call-done = bf16[4096,1,512]{0,2,1:T(8,128)(2,1)} async-done(((bf16[128,1,512]{0,2,1:T(8,128)(2,1)}), bf16[4096,1,512]{0,2,1:T(8,128)(2,1)}) %all-gather.3.cloned.1.call-update) | async-done | bytes 4194320 | tf_op jit(solution)/shard_map/all_gather | solution.py:72
  111.7 117.8 %while.20 = (s32[]{:T(128)}, f32[128,512]{0,1:T(8,128)S(1)}, s32[]{:T(128)}, bf16[32,2560]{1,0:T(8,128)(2,1)S(1)}, bf16[4096,512]{0,1:T(8,128)(2,1)}, /*index=5*...) while((s32[]{:T(128)}, f32[128,512]{0,1:T(8,128)S(1)}, s32[]{:T(128)}, ...), condition=%wide.region_3.0_spmd, body=%wide.region_0.0_spmd.sunk | while | flops 16842768 | bytes 17285120 | solution.py:50
  111.8 12.9 %conditional.2 = (f32[128,512]{0,1:T(8,128)S(1)}) conditional(s32[]{:T(128)} %convert_element_type.39, f32[128,512]{0,1:T(8,128)S(1)} %get-tuple-element.299, (s32[]{:T(128)}, bf16[32,2560]{1,0:T(8,128)(2,1)S(1)}, s32[]{:T(128)}, bf16[4096,512]{0,1:T(8,128)(2,1)}, f32[128,512]{0,1:T(8,128)S(1)}) %tuple.78), branch_computations={%region_1.0_spmd, %region_2.0_spmd} | conditional | flops 16842760 | bytes 17284898 | solution.py:43
  111.9 0.2 reverse
  112.1 0.9 constant_dynamic-slice_fusion
  113.2 1.2 copy.16
  114.6 7.8 %reshape.15 = bf16[32,128,255]{2,1,0:T(8,128)(2,1)} reshape(bf16[32,32640]{1,0:T(8,128)(2,1)S(1)} %slice.80) | data formatting | bytes 4177920 | tf_op jit(solution)/shard_map/while/body/eval_jaxpr/cond/branch_1_fun/reshape | solution.py:20
  122.3 2.3 fusion
  124.7 12.9 %conditional.2 = (f32[128,512]{0,1:T(8,128)S(1)}) conditional(s32[]{:T(128)} %convert_element_type.39, f32[128,512]{0,1:T(8,128)S(1)} %get-tuple-element.299, (s32[]{:T(128)}, bf16[32,2560]{1,0:T(8,128)(2,1)S(1)}, s32[]{:T(128)}, bf16[4096,512]{0,1:T(8,128)(2,1)}, f32[128,512]{0,1:T(8,128)S(1)}) %tuple.78), branch_computations={%region_1.0_spmd, %region_2.0_spmd} | conditional | flops 16842760 | bytes 17284898 | solution.py:43
  124.8 0.2 reverse
  125.1 0.9 constant_dynamic-slice_fusion
  126.2 1.2 copy.16
  127.5 7.8 %reshape.15 = bf16[32,128,255]{2,1,0:T(8,128)(2,1)} reshape(bf16[32,32640]{1,0:T(8,128)(2,1)S(1)} %slice.80) | data formatting | bytes 4177920 | tf_op jit(solution)/shard_map/while/body/eval_jaxpr/cond/branch_1_fun/reshape | solution.py:20
  135.3 2.3 fusion
  137.7 12.9 %conditional.2 = (f32[128,512]{0,1:T(8,128)S(1)}) conditional(s32[]{:T(128)} %convert_element_type.39, f32[128,512]{0,1:T(8,128)S(1)} %get-tuple-element.299, (s32[]{:T(128)}, bf16[32,2560]{1,0:T(8,128)(2,1)S(1)}, s32[]{:T(128)}, bf16[4096,512]{0,1:T(8,128)(2,1)}, f32[128,512]{0,1:T(8,128)S(1)}) %tuple.78), branch_computations={%region_1.0_spmd, %region_2.0_spmd} | conditional | flops 16842760 | bytes 17284898 | solution.py:43
  137.8 0.2 reverse
  138.1 0.9 constant_dynamic-slice_fusion
  139.2 1.2 copy.16
  140.5 7.8 %reshape.15 = bf16[32,128,255]{2,1,0:T(8,128)(2,1)} reshape(bf16[32,32640]{1,0:T(8,128)(2,1)S(1)} %slice.80) | data formatting | bytes 4177920 | tf_op jit(solution)/shard_map/while/body/eval_jaxpr/cond/branch_1_fun/reshape | solution.py:20
  148.3 2.3 fusion
  150.7 12.9 %conditional.2 = (f32[128,512]{0,1:T(8,128)S(1)}) conditional(s32[]{:T(128)} %convert_element_type.39, f32[128,512]{0,1:T(8,128)S(1)} %get-tuple-element.299, (s32[]{:T(128)}, bf16[32,2560]{1,0:T(8,128)(2,1)S(1)}, s32[]{:T(128)}, bf16[4096,512]{0,1:T(8,128)(2,1)}, f32[128,512]{0,1:T(8,128)S(1)}) %tuple.78), branch_computations={%region_1.0_spmd, %region_2.0_spmd} | conditional | flops 16842760 | bytes 17284898 | solution.py:43
  150.8 0.2 reverse
  151.1 0.9 constant_dynamic-slice_fusion
  152.1 1.2 copy.16
  153.5 7.8 %reshape.15 = bf16[32,128,255]{2,1,0:T(8,128)(2,1)} reshape(bf16[32,32640]{1,0:T(8,128)(2,1)S(1)} %slice.80) | data formatting | bytes 4177920 | tf_op jit(solution)/shard_map/while/body/eval_jaxpr/cond/branch_1_fun/reshape | solution.py:20
  161.3 2.3 fusion
  163.7 12.9 %conditional.2 = (f32[128,512]{0,1:T(8,128)S(1)}) conditional(s32[]{:T(128)} %convert_element_type.39, f32[128,512]{0,1:T(8,128)S(1)} %get-tuple-element.299, (s32[]{:T(128)}, bf16[32,2560]{1,0:T(8,128)(2,1)S(1)}, s32[]{:T(128)}, bf16[4096,512]{0,1:T(8,128)(2,1)}, f32[128,512]{0,1:T(8,128)S(1)}) %tuple.78), branch_computations={%region_1.0_spmd, %region_2.0_spmd} | conditional | flops 16842760 | bytes 17284898 | solution.py:43
  163.8 0.2 reverse
  164.0 0.9 constant_dynamic-slice_fusion
  165.1 1.2 copy.16
  166.5 7.8 %reshape.15 = bf16[32,128,255]{2,1,0:T(8,128)(2,1)} reshape(bf16[32,32640]{1,0:T(8,128)(2,1)S(1)} %slice.80) | data formatting | bytes 4177920 | tf_op jit(solution)/shard_map/while/body/eval_jaxpr/cond/branch_1_fun/reshape | solution.py:20
  174.2 2.3 fusion
  176.6 12.9 %conditional.2 = (f32[128,512]{0,1:T(8,128)S(1)}) conditional(s32[]{:T(128)} %convert_element_type.39, f32[128,512]{0,1:T(8,128)S(1)} %get-tuple-element.299, (s32[]{:T(128)}, bf16[32,2560]{1,0:T(8,128)(2,1)S(1)}, s32[]{:T(128)}, bf16[4096,512]{0,1:T(8,128)(2,1)}, f32[128,512]{0,1:T(8,128)S(1)}) %tuple.78), branch_computations={%region_1.0_spmd, %region_2.0_spmd} | conditional | flops 16842760 | bytes 17284898 | solution.py:43
  176.7 0.2 reverse
  177.0 0.9 constant_dynamic-slice_fusion
  178.1 1.2 copy.16
  179.4 7.8 %reshape.15 = bf16[32,128,255]{2,1,0:T(8,128)(2,1)} reshape(bf16[32,32640]{1,0:T(8,128)(2,1)S(1)} %slice.80) | data formatting | bytes 4177920 | tf_op jit(solution)/shard_map/while/body/eval_jaxpr/cond/branch_1_fun/reshape | solution.py:20
  187.2 2.3 fusion
  189.6 12.9 %conditional.2 = (f32[128,512]{0,1:T(8,128)S(1)}) conditional(s32[]{:T(128)} %convert_element_type.39, f32[128,512]{0,1:T(8,128)S(1)} %get-tuple-element.299, (s32[]{:T(128)}, bf16[32,2560]{1,0:T(8,128)(2,1)S(1)}, s32[]{:T(128)}, bf16[4096,512]{0,1:T(8,128)(2,1)}, f32[128,512]{0,1:T(8,128)S(1)}) %tuple.78), branch_computations={%region_1.0_spmd, %region_2.0_spmd} | conditional | flops 16842760 | bytes 17284898 | solution.py:43
  190.0 0.9 constant_dynamic-slice_fusion
  191.1 1.2 copy.16
  192.4 7.8 %reshape.15 = bf16[32,128,255]{2,1,0:T(8,128)(2,1)} reshape(bf16[32,32640]{1,0:T(8,128)(2,1)S(1)} %slice.80) | data formatting | bytes 4177920 | tf_op jit(solution)/shard_map/while/body/eval_jaxpr/cond/branch_1_fun/reshape | solution.py:20
  200.2 2.3 fusion
  202.6 12.9 %conditional.2 = (f32[128,512]{0,1:T(8,128)S(1)}) conditional(s32[]{:T(128)} %convert_element_type.39, f32[128,512]{0,1:T(8,128)S(1)} %get-tuple-element.299, (s32[]{:T(128)}, bf16[32,2560]{1,0:T(8,128)(2,1)S(1)}, s32[]{:T(128)}, bf16[4096,512]{0,1:T(8,128)(2,1)}, f32[128,512]{0,1:T(8,128)S(1)}) %tuple.78), branch_computations={%region_1.0_spmd, %region_2.0_spmd} | conditional | flops 16842760 | bytes 17284898 | solution.py:43
  203.0 0.9 constant_dynamic-slice_fusion
  204.0 1.2 copy.16
  205.4 7.8 %reshape.15 = bf16[32,128,255]{2,1,0:T(8,128)(2,1)} reshape(bf16[32,32640]{1,0:T(8,128)(2,1)S(1)} %slice.80) | data formatting | bytes 4177920 | tf_op jit(solution)/shard_map/while/body/eval_jaxpr/cond/branch_1_fun/reshape | solution.py:20
  213.2 2.3 fusion
  215.6 12.9 %conditional.2 = (f32[128,512]{0,1:T(8,128)S(1)}) conditional(s32[]{:T(128)} %convert_element_type.39, f32[128,512]{0,1:T(8,128)S(1)} %get-tuple-element.299, (s32[]{:T(128)}, bf16[32,2560]{1,0:T(8,128)(2,1)S(1)}, s32[]{:T(128)}, bf16[4096,512]{0,1:T(8,128)(2,1)}, f32[128,512]{0,1:T(8,128)S(1)}) %tuple.78), branch_computations={%region_1.0_spmd, %region_2.0_spmd} | conditional | flops 16842760 | bytes 17284898 | solution.py:43
  215.9 0.9 constant_dynamic-slice_fusion
  217.0 1.2 copy.16
  218.4 7.8 %reshape.15 = bf16[32,128,255]{2,1,0:T(8,128)(2,1)} reshape(bf16[32,32640]{1,0:T(8,128)(2,1)S(1)} %slice.80) | data formatting | bytes 4177920 | tf_op jit(solution)/shard_map/while/body/eval_jaxpr/cond/branch_1_fun/reshape | solution.py:20
  226.1 2.3 fusion
  229.5 6.0 %convolution_convert_fusion = bf16[128,8192]{1,0:T(8,128)(2,1)} fusion(bf16[512,8192]{1,0:T(8,128)(2,1)} %param.11, f32[128,512]{0,1:T(8,128)S(1)} %get-tuple-element.232, f32[128,3,512]{0,2,1:T(8,128)S(1)} %fusion.2), kind=kOutput, calls=%fused_computation.5 | convolution fusion | flops 1074921472 | bytes 11010048 | tf_op jit(solution)/shard_map/dot_general | solution.py:75
  235.6 140.2 %reduce-scatter.2.cloned.1.call-done = bf16[128,1024]{1,0:T(8,128)(2,1)} async-done(((bf16[128,8192]{1,0:T(8,128)(2,1)}), bf16[128,1024]{1,0:T(8,128)(2,1)}) %reduce-scatter.2.cloned.1.call-update) | async-done | bytes 262160 | tf_op jit(solution)/shard_map/reduce_scatter | solution.py:76
  (93 shorter events, 5.5 us)
Async XLA Ops:
  6.5 105.2 %all-gather.3.cloned.1.call-start = ((), (), s32[]{:S(2)}) async-start(), calls=%async_computation.2 | async-start | bytes 4325376 | tf_op jit(solution)/shard_map/all_gather | solution.py:72
  7.5 16.8 %collective-permute-start = (bf16[6,3,512]{0,2,1:T(8,128)(2,1)S(1)}, bf16[6,3,512]{0,2,1:T(8,128)(2,1)S(1)}, u32[]{:S(2)}, u32[]{:S(2)}) collective-permute-start(bf16[6,3,512]{0,2,1:T(8,128)(2,1)S(1)} %copy.7), channel_id=1, source_target_pairs={{0,8},{8,16},{16,24},{24,32},{32,40},{40,48},{48,56},{56,64},{64,7... | collective-permute-start | bytes 55304 | tf_op jit(solution)/shard_map/ppermute | solution.py:11
  24.7 3.8 copy-start
  28.4 347.4 %reduce-scatter.2.cloned.1.call-start = ((), (), s32[]{:S(2)}) async-start(), calls=%async_computation.1 | async-start | bytes 2359296 | tf_op jit(solution)/shard_map/reduce_scatter | solution.py:76
Sparse Core Ops, SparseCore 0:
  28.5 83.1 all-gather.2
  235.7 140.0 reduce-scatter.1
where the time goes:
time: 384 us; the launch traced here: 383 us
  waiting for transfers between devices  234 us (61%)
  local copies, waits for them, and re-layouts  98.2 us (26%)
  matrix products  26.7 us (7%)
  between operations  13.5 us (4%)
  other arithmetic  4.52 us (1%)
  starting transfers between devices  3.87 us (1%)
    reduce_scatter x1, waiting for transfers between devices, body(): lax.psum_scatter(partial_sum.astype(jnp.bfloat16), 'tp', scatter_dimensio...  140 us
    all_gather x1, waiting for transfers between devices, body(): lax.all_gather(values, 'ctx', axis=0, tiled=True)  83.2 us
    reshape x9, local copies, waits for them, and re-layouts, toeplitz_block(): skewed = tiled[:, :tok_rows * width].reshape(groups, tok_rows, width)  70 us
    dot_general x9, matrix products, block_term(): jnp.einsum('gts,sgi->tgi', matrix, grouped, preferred_element_type=jnp.fl...  20.7 us
    cond x27, local copies, waits for them, and re-layouts  13.1 us
    ppermute x1, waiting for transfers between devices, shifted(): return lax.ppermute(array, axis, pairs)  10.5 us
    dynamic_slice x9, local copies, waits for them, and re-layouts, one_block(): source = lax.dynamic_slice_in_dim(piece, index * block, block, 0)  8.29 us
  transfers between devices with their start and end apart: 3, of which 3 were waited for; matrix products, arithmetic and copies ran while one was open for 1% of the time, Pallas kernels for 0%

commit v1 on v0

--- a/solution.py
+++ b/solution.py
@@ -69,7 +69,13 @@
     padded_taps = jnp.concatenate([padding, long_filter, padding], axis=1)
     empty = jnp.zeros(values.shape, jnp.float32)
     mixed = add_blocks(
-        empty, lax.all_gather(values, "ctx", axis=0, tiled=True), padded_taps, my_start, reach
+        empty,
+        jnp.concatenate(
+            lax.all_to_all(jnp.stack([values] * lax.axis_size("ctx")), "ctx", 0, 0), axis=0
+        ),
+        padded_taps,
+        my_start,
+        reach,
     )
     hidden = (conved[:, 0, :] * mixed).astype(jnp.bfloat16)
     partial_sum = jnp.dot(hidden, out_weight, preferred_element_type=jnp.float32)

time: 384 us -> 419 us (1.091)
  local copies, waits for them, and re-layouts: 98.2 us -> 114 us
  waiting for transfers between devices: 234 us -> 245 us
  starting transfers between devices: 3.87 us -> 12.8 us
    all_to_all x0 -> x1, waiting for transfers between devices: none -> 92.8 us  [body(): lax.all_to_all(jnp.stack([values] * lax.axis_size('ctx')), 'ctx', 0, 0)]
    all_gather x1 -> x0, waiting for transfers between devices: 83.2 us -> none  [body(): lax.all_gather(values, 'ctx', axis=0, tiled=True)]
    all_to_all x0 -> x1, starting transfers between devices: none -> 8.92 us  [body(): lax.all_to_all(jnp.stack([values] * lax.axis_size('ctx')), 'ctx', 0, 0)]
    all_to_all x0 -> x1, local copies, waits for them, and re-layouts: none -> 6.5 us  [body(): lax.all_to_all(jnp.stack([values] * lax.axis_size('ctx')), 'ctx', 0, 0)]
    while x0 -> x1, local copies, waits for them, and re-layouts: none -> 6.41 us  [add_blocks(): return lax.fori_loop(0, count // block, one_block, total)]
where the time goes in v1:
time: 419 us; the launch traced here: 418 us
  waiting for transfers between devices  245 us (58%)
  local copies, waits for them, and re-layouts  114 us (27%)
  matrix products  26.8 us (6%)
  between operations  13.5 us (3%)
  starting transfers between devices  12.8 us (3%)
    reduce_scatter x1, waiting for transfers between devices, body(): lax.psum_scatter(partial_sum.astype(jnp.bfloat16), 'tp', scatter_dimensio...  141 us
    all_to_all x1, waiting for transfers between devices, body(): lax.all_to_all(jnp.stack([values] * lax.axis_size('ctx')), 'ctx', 0, 0)  92.8 us
    reshape x9, local copies, waits for them, and re-layouts, toeplitz_block(): skewed = tiled[:, :tok_rows * width].reshape(groups, tok_rows, width)  70 us
    dot_general x9, matrix products, block_term(): jnp.einsum('gts,sgi->tgi', matrix, grouped, preferred_element_type=jnp.fl...  20.7 us
    cond x27, local copies, waits for them, and re-layouts  13.1 us
    ppermute x1, waiting for transfers between devices, shifted(): return lax.ppermute(array, axis, pairs)  10.5 us
    all_to_all x1, starting transfers between devices, body(): lax.all_to_all(jnp.stack([values] * lax.axis_size('ctx')), 'ctx', 0, 0)  8.92 us
  transfers between devices with their start and end apart: 3, of which 3 were waited for; matrix products, arithmetic and copies ran while one was open for 1% of the time, Pallas kernels for 0%

profile of v1, /device:TPU:2, one launch (start us, length us, event | category | flops | bytes accessed | tf_op | source)
XLA Modules:
  0.0 417.6 jit_solution(1654953857427935169)
XLA Ops:
  6.5 0.7 slice.63
  7.3 0.3 copy.11
  7.5 3.8 collective-permute-start
  11.4 1.2 fusion.13
  12.6 1.2 copy.12
  13.9 10.5 %collective-permute-done = bf16[6,3,512]{0,2,1:T(8,128)(2,1)S(1)} collective-permute-done((bf16[6,3,512]{0,2,1:T(8,128)(2,1)S(1)}, bf16[6,3,512]{0,2,1:T(8,128)(2,1)S(1)}, u32[]{:S(2)}, u32[]{:S(2)}) %collective-permute-start) | collective-permute-done | bytes 18464 | tf_op jit(solution)/shard_map/ppermute | solution.py:11
  24.4 0.3 maximum_convert_fusion
  24.7 3.0 fusion.2
  27.7 2.9 stack.2
  30.6 8.9 %all-to-all-start = ((bf16[32,128,512]{1,2,0:T(8,128)(2,1)}), bf16[32,128,512]{1,2,0:T(8,128)(2,1)}, u32[]{:S(2)}, u32[]{:S(2)}) async-start(bf16[32,128,512]{1,2,0:T(8,128)(2,1)} %stack.2), calls=%async_computation | async-start | bytes 8388608 | tf_op jit(solution)/shard_map/all_to_all | solution.py:74
  39.7 92.8 %all-to-all-done = bf16[32,128,512]{1,2,0:T(8,128)(2,1)} async-done(((bf16[32,128,512]{1,2,0:T(8,128)(2,1)}), bf16[32,128,512]{1,2,0:T(8,128)(2,1)}, u32[]{:S(2)}, u32[]{:S(2)}) %all-to-all-start) | async-done | bytes 4194336 | tf_op jit(solution)/shard_map/all_to_all | solution.py:74
  132.5 6.5 %copy.13 = bf16[32,128,512]{2,1,0:T(8,128)(2,1)} copy(bf16[32,128,512]{1,2,0:T(8,128)(2,1)} %all-to-all-done) | data formatting | bytes 8388608 | tf_op jit(solution)/shard_map/all_to_all | solution.py:74
  139.0 6.4 %copy.14 = bf16[4096,512]{0,1:T(8,128)(2,1)} copy(bf16[4096,512]{1,0:T(8,128)(2,1)} %bitcast.37) | data formatting | bytes 8388608 | tf_op jit(solution)/shard_map/while | solution.py:50
  145.4 117.9 %while.20 = (s32[]{:T(128)}, f32[128,512]{0,1:T(8,128)S(1)}, s32[]{:T(128)}, bf16[32,2560]{1,0:T(8,128)(2,1)S(1)}, bf16[4096,512]{0,1:T(8,128)(2,1)}, /*index=5*...) while((s32[]{:T(128)}, f32[128,512]{0,1:T(8,128)S(1)}, s32[]{:T(128)}, ...), condition=%wide.region_3.0_spmd, body=%wide.region_0.0_spmd.sunk | while | flops 16842768 | bytes 17285120 | solution.py:50
  145.5 12.9 %conditional.2 = (f32[128,512]{0,1:T(8,128)S(1)}) conditional(s32[]{:T(128)} %convert_element_type.43, f32[128,512]{0,1:T(8,128)S(1)} %get-tuple-element.304, (s32[]{:T(128)}, bf16[32,2560]{1,0:T(8,128)(2,1)S(1)}, s32[]{:T(128)}, bf16[4096,512]{0,1:T(8,128)(2,1)}, f32[128,512]{0,1:T(8,128)S(1)}) %tuple.79), branch_computations={%region_1.0_spmd, %region_2.0_spmd} | conditional | flops 16842760 | bytes 17284898 | solution.py:43
  145.6 0.2 reverse
  145.8 0.9 constant_dynamic-slice_fusion
  146.9 1.2 copy.22
  148.3 7.8 %reshape.22 = bf16[32,128,255]{2,1,0:T(8,128)(2,1)} reshape(bf16[32,32640]{1,0:T(8,128)(2,1)S(1)} %slice.80) | data formatting | bytes 4177920 | tf_op jit(solution)/shard_map/while/body/eval_jaxpr/cond/branch_1_fun/reshape | solution.py:20
  156.0 2.3 fusion
  158.4 12.9 %conditional.2 = (f32[128,512]{0,1:T(8,128)S(1)}) conditional(s32[]{:T(128)} %convert_element_type.43, f32[128,512]{0,1:T(8,128)S(1)} %get-tuple-element.304, (s32[]{:T(128)}, bf16[32,2560]{1,0:T(8,128)(2,1)S(1)}, s32[]{:T(128)}, bf16[4096,512]{0,1:T(8,128)(2,1)}, f32[128,512]{0,1:T(8,128)S(1)}) %tuple.79), branch_computations={%region_1.0_spmd, %region_2.0_spmd} | conditional | flops 16842760 | bytes 17284898 | solution.py:43
  158.6 0.2 reverse
  158.8 0.9 constant_dynamic-slice_fusion
  159.9 1.2 copy.22
  161.2 7.8 %reshape.22 = bf16[32,128,255]{2,1,0:T(8,128)(2,1)} reshape(bf16[32,32640]{1,0:T(8,128)(2,1)S(1)} %slice.80) | data formatting | bytes 4177920 | tf_op jit(solution)/shard_map/while/body/eval_jaxpr/cond/branch_1_fun/reshape | solution.py:20
  169.0 2.3 fusion
  171.4 12.9 %conditional.2 = (f32[128,512]{0,1:T(8,128)S(1)}) conditional(s32[]{:T(128)} %convert_element_type.43, f32[128,512]{0,1:T(8,128)S(1)} %get-tuple-element.304, (s32[]{:T(128)}, bf16[32,2560]{1,0:T(8,128)(2,1)S(1)}, s32[]{:T(128)}, bf16[4096,512]{0,1:T(8,128)(2,1)}, f32[128,512]{0,1:T(8,128)S(1)}) %tuple.79), branch_computations={%region_1.0_spmd, %region_2.0_spmd} | conditional | flops 16842760 | bytes 17284898 | solution.py:43
  171.8 0.9 constant_dynamic-slice_fusion
  172.9 1.2 copy.22
  174.2 7.8 %reshape.22 = bf16[32,128,255]{2,1,0:T(8,128)(2,1)} reshape(bf16[32,32640]{1,0:T(8,128)(2,1)S(1)} %slice.80) | data formatting | bytes 4177920 | tf_op jit(solution)/shard_map/while/body/eval_jaxpr/cond/branch_1_fun/reshape | solution.py:20
  182.0 2.3 fusion
  184.4 12.9 %conditional.2 = (f32[128,512]{0,1:T(8,128)S(1)}) conditional(s32[]{:T(128)} %convert_element_type.43, f32[128,512]{0,1:T(8,128)S(1)} %get-tuple-element.304, (s32[]{:T(128)}, bf16[32,2560]{1,0:T(8,128)(2,1)S(1)}, s32[]{:T(128)}, bf16[4096,512]{0,1:T(8,128)(2,1)}, f32[128,512]{0,1:T(8,128)S(1)}) %tuple.79), branch_computations={%region_1.0_spmd, %region_2.0_spmd} | conditional | flops 16842760 | bytes 17284898 | solution.py:43
  184.5 0.2 reverse
  184.8 0.9 constant_dynamic-slice_fusion
  185.8 1.2 copy.22
  187.2 7.8 %reshape.22 = bf16[32,128,255]{2,1,0:T(8,128)(2,1)} reshape(bf16[32,32640]{1,0:T(8,128)(2,1)S(1)} %slice.80) | data formatting | bytes 4177920 | tf_op jit(solution)/shard_map/while/body/eval_jaxpr/cond/branch_1_fun/reshape | solution.py:20
  195.0 2.3 fusion
  197.4 12.9 %conditional.2 = (f32[128,512]{0,1:T(8,128)S(1)}) conditional(s32[]{:T(128)} %convert_element_type.43, f32[128,512]{0,1:T(8,128)S(1)} %get-tuple-element.304, (s32[]{:T(128)}, bf16[32,2560]{1,0:T(8,128)(2,1)S(1)}, s32[]{:T(128)}, bf16[4096,512]{0,1:T(8,128)(2,1)}, f32[128,512]{0,1:T(8,128)S(1)}) %tuple.79), branch_computations={%region_1.0_spmd, %region_2.0_spmd} | conditional | flops 16842760 | bytes 17284898 | solution.py:43
  197.8 0.9 constant_dynamic-slice_fusion
  198.8 1.2 copy.22
  200.2 7.8 %reshape.22 = bf16[32,128,255]{2,1,0:T(8,128)(2,1)} reshape(bf16[32,32640]{1,0:T(8,128)(2,1)S(1)} %slice.80) | data formatting | bytes 4177920 | tf_op jit(solution)/shard_map/while/body/eval_jaxpr/cond/branch_1_fun/reshape | solution.py:20
  208.0 2.3 fusion
  210.4 12.9 %conditional.2 = (f32[128,512]{0,1:T(8,128)S(1)}) conditional(s32[]{:T(128)} %convert_element_type.43, f32[128,512]{0,1:T(8,128)S(1)} %get-tuple-element.304, (s32[]{:T(128)}, bf16[32,2560]{1,0:T(8,128)(2,1)S(1)}, s32[]{:T(128)}, bf16[4096,512]{0,1:T(8,128)(2,1)}, f32[128,512]{0,1:T(8,128)S(1)}) %tuple.79), branch_computations={%region_1.0_spmd, %region_2.0_spmd} | conditional | flops 16842760 | bytes 17284898 | solution.py:43
  210.7 0.9 constant_dynamic-slice_fusion
  211.8 1.2 copy.22
  213.2 7.8 %reshape.22 = bf16[32,128,255]{2,1,0:T(8,128)(2,1)} reshape(bf16[32,32640]{1,0:T(8,128)(2,1)S(1)} %slice.80) | data formatting | bytes 4177920 | tf_op jit(solution)/shard_map/while/body/eval_jaxpr/cond/branch_1_fun/reshape | solution.py:20
  220.9 2.3 fusion
  223.3 12.9 %conditional.2 = (f32[128,512]{0,1:T(8,128)S(1)}) conditional(s32[]{:T(128)} %convert_element_type.43, f32[128,512]{0,1:T(8,128)S(1)} %get-tuple-element.304, (s32[]{:T(128)}, bf16[32,2560]{1,0:T(8,128)(2,1)S(1)}, s32[]{:T(128)}, bf16[4096,512]{0,1:T(8,128)(2,1)}, f32[128,512]{0,1:T(8,128)S(1)}) %tuple.79), branch_computations={%region_1.0_spmd, %region_2.0_spmd} | conditional | flops 16842760 | bytes 17284898 | solution.py:43
  223.7 0.9 constant_dynamic-slice_fusion
  224.8 1.2 copy.22
  226.1 7.8 %reshape.22 = bf16[32,128,255]{2,1,0:T(8,128)(2,1)} reshape(bf16[32,32640]{1,0:T(8,128)(2,1)S(1)} %slice.80) | data formatting | bytes 4177920 | tf_op jit(solution)/shard_map/while/body/eval_jaxpr/cond/branch_1_fun/reshape | solution.py:20
  233.9 2.3 fusion
  236.3 12.9 %conditional.2 = (f32[128,512]{0,1:T(8,128)S(1)}) conditional(s32[]{:T(128)} %convert_element_type.43, f32[128,512]{0,1:T(8,128)S(1)} %get-tuple-element.304, (s32[]{:T(128)}, bf16[32,2560]{1,0:T(8,128)(2,1)S(1)}, s32[]{:T(128)}, bf16[4096,512]{0,1:T(8,128)(2,1)}, f32[128,512]{0,1:T(8,128)S(1)}) %tuple.79), branch_computations={%region_1.0_spmd, %region_2.0_spmd} | conditional | flops 16842760 | bytes 17284898 | solution.py:43
  236.7 0.9 constant_dynamic-slice_fusion
  237.8 1.2 copy.22
  239.1 7.8 %reshape.22 = bf16[32,128,255]{2,1,0:T(8,128)(2,1)} reshape(bf16[32,32640]{1,0:T(8,128)(2,1)S(1)} %slice.80) | data formatting | bytes 4177920 | tf_op jit(solution)/shard_map/while/body/eval_jaxpr/cond/branch_1_fun/reshape | solution.py:20
  246.9 2.3 fusion
  249.3 12.9 %conditional.2 = (f32[128,512]{0,1:T(8,128)S(1)}) conditional(s32[]{:T(128)} %convert_element_type.43, f32[128,512]{0,1:T(8,128)S(1)} %get-tuple-element.304, (s32[]{:T(128)}, bf16[32,2560]{1,0:T(8,128)(2,1)S(1)}, s32[]{:T(128)}, bf16[4096,512]{0,1:T(8,128)(2,1)}, f32[128,512]{0,1:T(8,128)S(1)}) %tuple.79), branch_computations={%region_1.0_spmd, %region_2.0_spmd} | conditional | flops 16842760 | bytes 17284898 | solution.py:43
  249.7 0.9 constant_dynamic-slice_fusion
  250.8 1.2 copy.22
  252.1 7.8 %reshape.22 = bf16[32,128,255]{2,1,0:T(8,128)(2,1)} reshape(bf16[32,32640]{1,0:T(8,128)(2,1)S(1)} %slice.80) | data formatting | bytes 4177920 | tf_op jit(solution)/shard_map/while/body/eval_jaxpr/cond/branch_1_fun/reshape | solution.py:20
  259.9 2.3 fusion
  263.3 6.0 %convolution_convert_fusion = bf16[128,8192]{1,0:T(8,128)(2,1)} fusion(bf16[512,8192]{1,0:T(8,128)(2,1)} %param.11, f32[128,512]{0,1:T(8,128)S(1)} %get-tuple-element.232, f32[128,3,512]{0,2,1:T(8,128)S(1)} %fusion.2), kind=kOutput, calls=%fused_computation.5 | convolution fusion | flops 1074921472 | bytes 11010048 | tf_op jit(solution)/shard_map/dot_general | solution.py:81
  269.4 141.4 %reduce-scatter.2.cloned.1.call-done = bf16[128,1024]{1,0:T(8,128)(2,1)} async-done(((bf16[128,8192]{1,0:T(8,128)(2,1)}), bf16[128,1024]{1,0:T(8,128)(2,1)}) %reduce-scatter.2.cloned.1.call-update) | async-done | bytes 262160 | tf_op jit(solution)/shard_map/reduce_scatter | solution.py:82
  (95 shorter events, 6.0 us)
Async XLA Ops:
  7.5 16.8 %collective-permute-start = (bf16[6,3,512]{0,2,1:T(8,128)(2,1)S(1)}, bf16[6,3,512]{0,2,1:T(8,128)(2,1)S(1)}, u32[]{:S(2)}, u32[]{:S(2)}) collective-permute-start(bf16[6,3,512]{0,2,1:T(8,128)(2,1)S(1)} %copy.11), channel_id=1, source_target_pairs={{0,8},{8,16},{16,24},{24,32},{32,40},{40,48},{48,56},{56,64},{64,7... | collective-permute-start | bytes 55304 | tf_op jit(solution)/shard_map/ppermute | solution.py:11
  30.6 9.0 %copy-start = (bf16[32,2048]{1,0:T(8,128)(2,1)S(1)}, bf16[32,2048]{1,0:T(8,128)(2,1)}, u32[]{:S(2)}) copy-start(bf16[32,2048]{1,0:T(8,128)(2,1)} %param.10) | copy-start | bytes 393220
  30.6 101.9 %all-to-all-start = ((bf16[32,128,512]{1,2,0:T(8,128)(2,1)}), bf16[32,128,512]{1,2,0:T(8,128)(2,1)}, u32[]{:S(2)}, u32[]{:S(2)}) async-start(bf16[32,128,512]{1,2,0:T(8,128)(2,1)} %stack.2), calls=%async_computation | async-start | bytes 8388608 | tf_op jit(solution)/shard_map/all_to_all | solution.py:74
  39.6 371.2 %reduce-scatter.2.cloned.1.call-start = ((), (), s32[]{:S(2)}) async-start(), calls=%async_computation.2 | async-start | bytes 2359296 | tf_op jit(solution)/shard_map/reduce_scatter | solution.py:82
Sparse Core Ops, SparseCore 0:
  269.5 141.2 reduce-scatter.1
